TPU v7x, 512 devices: a whole 4x4x16 slice. The times are simulated.
512 devices in a mesh: tm: 128 (over z, y, core), batch: 4 (over x).
Axes of the slice: x: 4, y: 4, z: 16, core: 2. Of those that a mesh axis runs over, the one named last changes fastest.
Arguments:
- inputs: bfloat16 [4096, 4, 128], P('tm', 'batch'), may hold values from -6 to 6
- h_start: float32 [4, 128], P('batch'), may hold values from -4 to 4
- in_weight: bfloat16 [128, 384], replicated, may hold values from -0.5 to 0.5
- rec_weight: float32 [128, 384], replicated, may hold values from -0.5 to 0.5
- update_bias: float32 [128], replicated, may hold values from -1 to 14
- reset_bias: float32 [128], replicated, may hold values from -4 to 4
- cand_bias: float32 [128], replicated, may hold values from -3 to 3
- rec_bias: float32 [128], replicated, may hold values from -3 to 3
Outputs:
- states: float32 [4096, 4, 128], P('tm', 'batch')
- residual_norms: float32 [2], replicated
All inputs are finite; a program needn't handle non-finite values.
Results may differ from a plain program's by a relative error of at most 0.0003.
Values sent between devices are 32-bit elements; how exact they have to be, the bound alone decides.
A program may use at most 64 MiB of HBM per device.

v0:
```python
import jax
import jax.numpy as jnp
from jax import lax
from jax.sharding import PartitionSpec as P

ITERS = 2
BLOCK = 16


HIGH = lax.Precision.HIGHEST


def passed_along(shard, axis, by):
    peers = lax.axis_size(axis)
    pairs = [(i, i + by) for i in range(peers) if 0 <= i + by < peers]
    return lax.ppermute(shard, axis, pairs)


def cell_parts(in_gates, previous, rec_weight, update_bias, reset_bias, cand_bias, rec_bias):
    units = rec_weight.shape[0]
    rec_gates = jnp.dot(previous, rec_weight, precision=HIGH)
    update_gate = jax.nn.sigmoid(in_gates[:, :units] + rec_gates[:, :units] + update_bias)
    reset_gate = jax.nn.sigmoid(
        in_gates[:, units : 2 * units] + rec_gates[:, units : 2 * units] + reset_bias
    )
    recur_term = rec_gates[:, 2 * units :] + rec_bias
    candidate = jnp.tanh(in_gates[:, 2 * units :] + cand_bias + reset_gate * recur_term)
    stepped = (1.0 - update_gate) * candidate + update_gate * previous
    return (update_gate, reset_gate, recur_term, candidate, stepped)


def jacobian(previous, update_gate, reset_gate, recur_term, candidate, rec_weight, identity):
    units = rec_weight.shape[0]
    coef_update = (previous - candidate) * update_gate * (1.0 - update_gate)
    common = (1.0 - update_gate) * (1.0 - candidate * candidate)
    coef_cand = common * reset_gate
    coef_reset = common * recur_term * reset_gate * (1.0 - reset_gate)
    return (
        identity * update_gate[..., None, :]
        + rec_weight[:, :units] * coef_update[..., None, :]
        + rec_weight[:, units : 2 * units] * coef_reset[..., None, :]
        + rec_weight[:, 2 * units :] * coef_cand[..., None, :]
    )


def combine(earlier, later):
    mat_early, vec_early = earlier
    mat_late, vec_late = later
    new_mat = jnp.einsum("...ij,...jk->...ik", mat_early, mat_late, precision=HIGH)
    new_vec = jnp.einsum("...j,...jk->...k", vec_early, mat_late, precision=HIGH) + vec_late
    return (new_mat, new_vec)


def solve_chain(mats, vecs, start, is_first, identity):
    step_count, units = vecs.shape
    blocks = step_count // BLOCK
    blk_mats = mats.reshape(blocks, BLOCK, units, units)
    blk_vecs = vecs.reshape(blocks, BLOCK, units)
    fold_mats, fold_vecs = (blk_mats, blk_vecs)
    while fold_mats.shape[1] > 1:
        fold_mats, fold_vecs = combine(
            (fold_mats[:, 0::2], fold_vecs[:, 0::2]), (fold_mats[:, 1::2], fold_vecs[:, 1::2])
        )
    fold_mats = fold_mats[:, 0]
    fold_vecs = fold_vecs[:, 0]
    incl_mats, incl_vecs = lax.associative_scan(combine, (fold_mats, fold_vecs), axis=0)
    whole_mat = incl_mats[-1]
    whole_vec = incl_vecs[-1]

    def relay(index, carried):
        leaving = jnp.dot(carried, whole_mat, precision=HIGH) + whole_vec
        arrived = passed_along(leaving, "tm", 1)
        return jnp.where(is_first, start, arrived)

    entering = lax.fori_loop(0, lax.axis_size("tm"), relay, start)
    excl_mats = jnp.concatenate([identity[None], incl_mats[:-1]], axis=0)
    excl_vecs = jnp.concatenate([jnp.zeros((1, units), jnp.float32), incl_vecs[:-1]], axis=0)
    block_starts = jnp.einsum("j,bjk->bk", entering, excl_mats, precision=HIGH) + excl_vecs

    def advance(carried, item):
        one_mat, one_vec = item
        carried = jnp.einsum("bj,bjk->bk", carried, one_mat, precision=HIGH) + one_vec
        return (carried, carried)

    final_rows, walked = lax.scan(
        advance, block_starts, (jnp.moveaxis(blk_mats, 1, 0), jnp.moveaxis(blk_vecs, 1, 0))
    )
    return jnp.moveaxis(walked, 0, 1).reshape(step_count, units)


def per_device(
    inputs, h_start, in_weight, rec_weight, update_bias, reset_bias, cand_bias, rec_bias
):
    step_count = inputs.shape[0]
    units = rec_weight.shape[0]
    is_first = lax.axis_index("tm") == 0
    start = h_start[0]
    identity = jnp.eye(units, dtype=jnp.float32)
    in_gates = jnp.dot(inputs[:, 0, :], in_weight, preferred_element_type=jnp.float32)
    total_steps = step_count * lax.axis_size("tm")
    position = lax.axis_index("tm") * step_count + jnp.arange(step_count, dtype=jnp.int32)
    weights = (position.astype(jnp.float32) + 1.0) / total_steps
    first_row = jnp.where(is_first, start, jnp.zeros_like(start))
    previous = jnp.zeros((step_count, units), jnp.float32).at[0].set(first_row)
    current = previous
    partials = []

    def record(current, stepped):
        local_sum = jnp.sum(weights[:, None] * (current - stepped) ** 2)
        return lax.psum(local_sum, ("tm", "batch"))

    for newton in range(ITERS):
        update_gate, reset_gate, recur_term, candidate, stepped = cell_parts(
            in_gates, previous, rec_weight, update_bias, reset_bias, cand_bias, rec_bias
        )
        if newton > 0:
            partials.append(record(current, stepped))
        mats = jacobian(
            previous, update_gate, reset_gate, recur_term, candidate, rec_weight, identity
        )
        offsets = stepped - jnp.einsum("tj,tjk->tk", previous, mats, precision=HIGH)
        current = solve_chain(mats, offsets, start, is_first, identity)
        arrived = passed_along(current[-1], "tm", 1)
        previous = jnp.concatenate(
            [jnp.where(is_first, start, arrived)[None, :], current[:-1]], axis=0
        )
    parts = cell_parts(in_gates, previous, rec_weight, update_bias, reset_bias, cand_bias, rec_bias)
    partials.append(record(current, parts[4]))
    totals = jnp.stack(partials)
    denom = lax.axis_size("batch") * units * (total_steps + 1) / 2.0
    residual_norms = jnp.sqrt(totals / denom + 1e-06)
    return (current[:, None, :], residual_norms)


def solution(mesh):
    in_specs = (P("tm", "batch", None), P("batch", None), P(), P(), P(), P(), P(), P())
    out_specs = (P("tm", "batch", None), P())
    return jax.shard_map(
        per_device, mesh=mesh, in_specs=in_specs, out_specs=out_specs, check_vma=False
    )
```

profile of v0, /device:TPU:1, one launch (start us, length us, event | category | flops | bytes accessed | tf_op | source)
XLA Modules:
  0.0 2293.7 jit_solution(8528471653368189477)
XLA Ops:
  13.2 925.3 %while.45 = (s32[]{:T(128)}, f32[128]{0:T(128)S(1)}, pred[]{:T(512)}, f32[128,128]{1,0:T(8,128)S(1)}, f32[128]{0:T(128)S(1)}, /*index=5*/f32[128]{0:T(128)S(1)}, s32[]{:T(128)}) while((s32[]{:T(128)}, f32[128]{0:T(128)S(1)}, pred[]{:T(512)}, f32[128,128]{1,0:T(8,128)S(1)}, f32[128]{0:T(128)S(1)}, /*index=5*/f32[128]{0:T(128)S(1)}, ...), condition=%wide.region_1.2_spmd, body=%wide.region_0.1_spmd.sunk | while | flops 196866 | bytes 70774 | solution.py:75
  705.0 7.5 collective-permute-start
  713.3 7.5 collective-permute-start
  721.7 7.5 collective-permute-start
  730.0 7.5 collective-permute-start
  738.4 7.5 collective-permute-start
  746.7 7.5 collective-permute-start
  755.1 7.5 collective-permute-start
  763.4 7.5 collective-permute-start
  771.8 7.5 collective-permute-start
  780.1 7.5 collective-permute-start
  788.5 7.5 collective-permute-start
  796.8 7.5 collective-permute-start
  805.1 7.5 collective-permute-start
  813.5 7.5 collective-permute-start
  821.8 7.5 collective-permute-start
  830.2 7.5 collective-permute-start
  838.5 7.5 collective-permute-start
  846.9 7.5 collective-permute-start
  855.2 7.5 collective-permute-start
  863.6 7.5 collective-permute-start
  871.9 7.5 collective-permute-start
  880.3 7.5 collective-permute-start
  888.6 7.5 collective-permute-start
  896.9 7.5 collective-permute-start
  905.3 7.5 collective-permute-start
  913.6 7.5 collective-permute-start
  922.0 7.5 collective-permute-start
  930.3 7.5 collective-permute-start
  943.2 7.7 collective-permute-start.2
  959.8 1068.3 %while.47 = (s32[]{:T(128)}, f32[128]{0:T(128)S(1)}, pred[]{:T(512)}, f32[128,128]{1,0:T(8,128)S(1)}, f32[128]{0:T(128)S(1)}, /*index=5*/f32[128]{0:T(128)S(1)}, s32[]{:T(128)}) while((s32[]{:T(128)}, f32[128]{0:T(128)S(1)}, pred[]{:T(512)}, f32[128,128]{1,0:T(8,128)S(1)}, f32[128]{0:T(128)S(1)}, /*index=5*/f32[128]{0:T(128)S(1)}, ...), condition=%wide.region_5.6_spmd, body=%wide.region_4.5_spmd.sunk | while | flops 196866 | bytes 70774 | solution.py:75
  960.0 7.5 collective-permute-start.1
  968.3 7.5 collective-permute-start.1
  976.7 7.5 collective-permute-start.1
  985.0 7.5 collective-permute-start.1
  993.4 7.5 collective-permute-start.1
  1010.1 7.5 collective-permute-start.1
  1026.8 7.5 collective-permute-start.1
  1043.5 7.5 collective-permute-start.1
  1068.5 7.5 collective-permute-start.1
  1085.2 7.5 collective-permute-start.1
  1101.9 7.5 collective-permute-start.1
  1110.2 7.5 collective-permute-start.1
  1118.6 7.5 collective-permute-start.1
  1126.9 7.5 collective-permute-start.1
  1143.6 7.5 collective-permute-start.1
  1160.3 7.5 collective-permute-start.1
  1177.0 7.5 collective-permute-start.1
  1202.0 7.5 collective-permute-start.1
  1218.7 7.5 collective-permute-start.1
  1227.1 7.5 collective-permute-start.1
  1235.4 7.5 collective-permute-start.1
  1243.8 7.5 collective-permute-start.1
  1252.1 7.5 collective-permute-start.1
  1260.5 7.5 collective-permute-start.1
  1268.8 7.5 collective-permute-start.1
  1277.2 7.5 collective-permute-start.1
  1285.5 7.5 collective-permute-start.1
  1293.8 7.5 collective-permute-start.1
  1302.2 7.5 collective-permute-start.1
  1310.5 7.5 collective-permute-start.1
  1318.9 7.5 collective-permute-start.1
  1327.2 7.5 collective-permute-start.1
  2042.0 249.8 %all-reduce.9 = (f32[1]{0:T(128)}, f32[1]{0:T(128)}) all-reduce(f32[1]{0:T(128)} %bitcast.126, f32[1]{0:T(128)} %bitcast.122), channel_id=1, replica_groups=mesh['tm'=128,'batch'=4] {'tm','batch'}, use_global_device_ids=true, to_apply=%region_11.12 | all-reduce | flops 2 | bytes 16 | tf_op jit(solution)/shard_map/psum | solution.py:110
  (1147 shorter events, 1591.6 us)
Async XLA Ops:
  13.3 9.4 collective-permute-start
  713.3 8.2 collective-permute-start
  730.0 8.2 collective-permute-start
  746.7 8.2 collective-permute-start
  763.4 8.2 collective-permute-start
  805.1 8.2 collective-permute-start
  821.8 8.2 collective-permute-start
  838.5 8.2 collective-permute-start
  855.2 8.2 collective-permute-start
  871.9 8.2 collective-permute-start
  888.6 8.2 collective-permute-start
  905.3 8.2 collective-permute-start
  922.0 8.2 collective-permute-start
  960.0 8.2 collective-permute-start.1
  968.3 8.2 collective-permute-start.1
  993.4 8.2 collective-permute-start.1
  1010.1 8.2 collective-permute-start.1
  1026.8 8.2 collective-permute-start.1
  1043.5 8.2 collective-permute-start.1
  1068.5 8.2 collective-permute-start.1
  1085.2 8.2 collective-permute-start.1
  1101.9 8.2 collective-permute-start.1
  1118.6 8.2 collective-permute-start.1
  1126.9 8.2 collective-permute-start.1
  1143.6 8.2 collective-permute-start.1
  1160.3 8.2 collective-permute-start.1
  1177.0 8.2 collective-permute-start.1
  1202.0 8.2 collective-permute-start.1
  1227.1 8.2 collective-permute-start.1
  1235.4 8.2 collective-permute-start.1
  1268.8 8.2 collective-permute-start.1
  1277.2 8.2 collective-permute-start.1
  1310.5 8.2 collective-permute-start.1
  1318.9 8.2 collective-permute-start.1
  1343.9 8.2 collective-permute-start.1
  1352.3 8.2 collective-permute-start.1
  1385.7 8.2 collective-permute-start.1
  1394.0 8.2 collective-permute-start.1
  1427.4 8.2 collective-permute-start.1
  1435.7 8.2 collective-permute-start.1
  1469.1 8.2 collective-permute-start.1
  1477.5 8.2 collective-permute-start.1
  1502.5 8.2 collective-permute-start.1
  1510.8 8.2 collective-permute-start.1
  1544.2 8.2 collective-permute-start.1
  1552.6 8.2 collective-permute-start.1
  1586.0 8.2 collective-permute-start.1
  1594.3 8.2 collective-permute-start.1
  1627.7 8.2 collective-permute-start.1
  1636.0 8.2 collective-permute-start.1
  1661.1 8.2 collective-permute-start.1
  1669.4 8.2 collective-permute-start.1
  1702.8 8.2 collective-permute-start.1
  1711.2 8.2 collective-permute-start.1
  1744.5 8.2 collective-permute-start.1
  1752.9 8.2 collective-permute-start.1
  1786.3 8.2 collective-permute-start.1
  1794.6 8.2 collective-permute-start.1
  1819.7 8.2 collective-permute-start.1
  1828.0 8.2 collective-permute-start.1
  1861.4 8.2 collective-permute-start.1
  1869.7 8.2 collective-permute-start.1
  1903.1 8.2 collective-permute-start.1
  1911.5 8.2 collective-permute-start.1
  (203 other events, 6405.7 us)
where the time goes:
time: 2300 us; the launch traced here: 2290 us
  starting transfers between devices  1780 us (77%)
  blocking collectives  250 us (11%)
  waiting for transfers between devices  185 us (8%)
  matrix products  63.5 us (3%)
    ppermute x258, starting transfers between devices, passed_along(): return lax.ppermute(shard, axis, pairs)  1780 us
    psum x1, blocking collectives, record(): return lax.psum(local_sum, ('tm', 'batch'))  250 us
    ppermute x258, waiting for transfers between devices, passed_along(): return lax.ppermute(shard, axis, pairs)  185 us
  transfers between devices with their start and end apart: 258, of which 258 were waited for; matrix products, arithmetic and copies ran while one was open for 0% of the time, Pallas kernels for 0%

commit v1 on v0

v1 whole, which is shorter than its diff:
```python
import functools
import jax
import jax.numpy as jnp
from jax import lax
from jax.experimental import pallas as pl
from jax.experimental.pallas import tpu as pltpu
from jax.sharding import PartitionSpec as P

ITERS = 2
BLOCKS = 4
PLANE = 8
ZROUNDS = 1
H = 128
ROWS = H + 8
F32 = jnp.float32
BF16 = jnp.bfloat16


def split(value):
    high = value.astype(BF16)
    low = (value - high.astype(F32)).astype(BF16)
    return high, low


def split_dot(left, right):
    left_high, left_low = split(left)
    right_high, right_low = split(right)
    width = right.shape[1]
    both = jnp.concatenate([right_high, right_low], axis=1)
    out = jnp.dot(
        jnp.concatenate([left_high, left_low], axis=1),
        jnp.concatenate([both, both], axis=0),
        preferred_element_type=F32,
    )
    return out[:, :width] + out[:, width:]


def compose(early, late):
    return early + late + split_dot(early, late[:H])


def kernel(
    nz, nx,
    x_ref, start_ref, in_w_ref, rec_w_ref, ub_ref, rb_ref, cb_ref, nb_ref,
    out_ref, norm_ref,
    gx, coef, offs, prefix, own, got, acc, zown, zgot, hvec, hgot, hbuf, heads,
    part_a, part_b, part_c,
    m_send, m_recv, z_send, z_recv, h_send, h_recv,
    a_send, a_recv, b_send, b_recv, c_send, c_recv,
):
    steps = x_ref.shape[0]
    length = steps // BLOCKS
    me = lax.axis_index("tm")
    col = lax.axis_index("batch")
    z = me // PLANE
    inner = me % PLANE
    y = inner // 2
    core = inner % 2

    mates = (
        z * PLANE + y * 2 + (1 - core),
        z * PLANE + (y + 1 - 2 * (y % 2)) * 2 + core,
        z * PLANE + (3 - y) * 2 + core,
    )
    uppers = (core == 1, y % 2 == 1, y >= 2)

    barrier = pltpu.get_barrier_semaphore()

    def hello(**where):
        pl.semaphore_signal(
            barrier, inc=1, device_id=where, device_id_type=pl.DeviceIdType.MESH
        )

    for j in range(1, PLANE):
        hello(tm=z * PLANE + (inner + j) % PLANE)
    for j in range(1, nz):
        hello(tm=((z + j) % nz) * PLANE + inner)
    for j in range(1, nx):
        hello(batch=(col + j) % nx)

    eye = (
        lax.broadcasted_iota(jnp.int32, (H, H), 0)
        == lax.broadcasted_iota(jnp.int32, (H, H), 1)
    ).astype(F32)

    def apply(row, mapped):
        column = jnp.sum(eye * row[:1], axis=1, keepdims=True)
        moved = jnp.sum(column * mapped[:H], axis=0, keepdims=True)
        return row + jnp.broadcast_to(moved + mapped[H : H + 1], row.shape)

    def push(src, dst, ssem, rsem, **where):
        return pltpu.make_async_remote_copy(
            src_ref=src, dst_ref=dst, send_sem=ssem, recv_sem=rsem,
            device_id=where, device_id_type=pl.DeviceIdType.MESH,
        )

    gx[...] = jnp.dot(x_ref[...], in_w_ref[...], preferred_element_type=F32)
    start = jnp.broadcast_to(start_ref[...], (8, H))
    weight = (
        (me * steps + lax.broadcasted_iota(jnp.int32, (steps, 1), 0)).astype(F32) + 1.0
    ) / (steps * nz * PLANE)

    def cell(prev):
        gh = split_dot(prev, rec_w_ref[...])
        update = jax.nn.sigmoid(gx[:, :H] + gh[:, :H] + ub_ref[...])
        reset = jax.nn.sigmoid(gx[:, H : 2 * H] + gh[:, H : 2 * H] + rb_ref[...])
        recur = gh[:, 2 * H :] + nb_ref[...]
        cand = jnp.tanh(gx[:, 2 * H :] + cb_ref[...] + reset * recur)
        stepped = (1.0 - update) * cand + update * prev
        return gh, update, reset, recur, cand, stepped

    first = jnp.where(me == 0, start_ref[...], jnp.zeros((1, H), F32))
    prev = jnp.where(
        lax.broadcasted_iota(jnp.int32, (steps, H), 0) == 0,
        jnp.broadcast_to(first, (steps, H)),
        jnp.zeros((steps, H), F32),
    )
    current = prev
    sums = []

    for it in range(ITERS):
        gh, update, reset, recur, cand, stepped = cell(prev)
        if it > 0:
            sums.append(
                jnp.sum(weight * (current - stepped) ** 2, axis=0, keepdims=True)
            )
        c_update = (prev - cand) * update * (1.0 - update)
        common = (1.0 - update) * (1.0 - cand * cand)
        c_cand = common * reset
        c_reset = common * recur * reset * (1.0 - reset)
        coef[0] = c_update
        coef[1] = c_reset
        coef[2] = c_cand
        coef[3] = update - 1.0
        offs[...] = stepped - (
            update * prev
            + c_update * gh[:, :H]
            + c_reset * gh[:, H : 2 * H]
            + c_cand * gh[:, 2 * H :]
        )

        def step_matrix(t):
            at = pl.ds(t, 1)
            return (
                rec_w_ref[:, :H] * coef[0, at, :]
                + rec_w_ref[:, H : 2 * H] * coef[1, at, :]
                + rec_w_ref[:, 2 * H :] * coef[2, at, :]
                + eye * coef[3, at, :]
            )

        pad_row = lax.broadcasted_iota(jnp.int32, (8, H), 0) == 0

        def step_tail(t):
            return jnp.where(
                pad_row, jnp.broadcast_to(offs[pl.ds(t, 1), :], (8, H)), 0.0
            )

        for b in range(BLOCKS):
            prefix[b, 0, :H] = step_matrix(b * length)
            prefix[b, 0, H:] = step_tail(b * length)

        def extend(t, carry):
            for b in range(BLOCKS):
                before = prefix[b, t - 1]
                late = step_matrix(b * length + t)
                more = split_dot(before, late)
                prefix[b, t, :H] = before[:H] + late + more[:H]
                prefix[b, t, H:] = before[H:] + step_tail(b * length + t) + more[H:]
            return carry

        lax.fori_loop(1, length, extend, 0)

        last = length - 1
        heads[1] = prefix[0, last]
        heads[2] = compose(prefix[0, last], prefix[1, last])
        tail_pair = compose(prefix[2, last], prefix[3, last])
        own[it, 0] = compose(heads[2], tail_pair)

        if it == 0:
            pl.semaphore_wait(barrier, (PLANE - 1) + (nz - 1) + (nx - 1))

        copies = []
        for k in range(3):
            copy = push(
                own.at[it, k], got.at[it, k], m_send.at[it, k], m_recv.at[it, k],
                tm=mates[k],
            )
            copy.start()
            copies.append(copy)
            if k == 0:
                heads[3] = compose(heads[2], prefix[2, last])
            copy.wait_recv()
            mine = own[it, k]
            theirs = got[it, k]
            early = jnp.where(uppers[k], theirs, mine)
            late = jnp.where(uppers[k], mine, theirs)
            merged = compose(early, late)
            if k < 2:
                own[it, k + 1] = merged
            else:
                zown[it, 0] = merged

        h_copy_out = []

        def relay(to, level, valid):
            @pl.when(valid)
            def _():
                hvec[it, 1 + level] = apply(hvec[it, 0], zown[it, level])
                push(
                    hvec.at[it, 1 + level], hgot.at[it],
                    h_send.at[it, level], h_recv.at[it],
                    tm=jnp.minimum(z + to, nz - 1) * PLANE + inner,
                ).start()
            h_copy_out.append((to, level, valid))

        def receive(valid):
            @pl.when(valid)
            def _():
                push(
                    hgot.at[it], hgot.at[it], h_send.at[it, 0], h_recv.at[it],
                    tm=me,
                ).wait_recv()
                hvec[it, 0] = hgot[it]

        @pl.when(z == 0)
        def _():
            hvec[it, 0] = start

        z_out = []
        for k in range(ZROUNDS):
            d = 1 << k

            @pl.when(z >= d)
            def _():
                push(
                    zown.at[it, k], zgot.at[it, k], z_send.at[it, k], z_recv.at[it, k],
                    tm=(jnp.maximum(z - d, 0)) * PLANE + inner,
                ).start()

            z_out.append(d)
            if k > 0:
                receive((z >= d // 2) & (z < d))
            relay(d, k, z < d)

            @pl.when(z + d < nz)
            def _():
                push(
                    zown.at[it, k], zgot.at[it, k], z_send.at[it, k], z_recv.at[it, k],
                    tm=me,
                ).wait_recv()
                zown[it, k + 1] = compose(zown[it, k], zgot[it, k])

        wide = 1 << ZROUNDS
        known = 1 if ZROUNDS == 0 else wide // 2

        zero = jnp.zeros((ROWS, H), F32)

        def inner_map():
            lead = jnp.where(uppers[2], got[it, 2], zero)
            acc[0] = compose(lead, jnp.where(uppers[1], got[it, 1], zero))
            acc[1] = compose(acc[0], jnp.where(uppers[0], got[it, 0], zero))
            for b in range(1, BLOCKS):
                acc[1 + b] = compose(acc[1], heads[b])

        @pl.when(z < known)
        def _():
            @pl.when(z + wide < nz)
            def _():
                hvec[it, 1 + ZROUNDS] = apply(hvec[it, 0], zown[it, ZROUNDS])
                push(
                    hvec.at[it, 1 + ZROUNDS], hgot.at[it],
                    h_send.at[it, ZROUNDS], h_recv.at[it],
                    tm=jnp.minimum(z + wide, nz - 1) * PLANE + inner,
                ).start()

        inner_map()
        receive(z >= known)
        relay(wide, ZROUNDS, (z >= known) & (z + wide < nz))

        entering = hvec[it, 0]
        at_device = apply(entering, acc[1])
        hbuf[0:8] = at_device
        for b in range(BLOCKS):
            head = at_device if b == 0 else apply(entering, acc[1 + b])
            column = jnp.sum(eye * head[:1], axis=1, keepdims=True)
            rows = []
            for t in range(length):
                moved = jnp.sum(column * prefix[b, t, :H], axis=0, keepdims=True)
                rows.append(moved + prefix[b, t, H : H + 1] + head[:1])
            hbuf[8 + b * length : 8 + (b + 1) * length] = jnp.concatenate(rows, axis=0)
        current = hbuf[8 : 8 + steps]
        prev = hbuf[7 : 7 + steps]

        for k in range(3):
            copies[k].wait_send()
        for k, d in enumerate(z_out):
            @pl.when(z >= d)
            def _():
                push(
                    zown.at[it, k], zgot.at[it, k], z_send.at[it, k], z_recv.at[it, k],
                    tm=me,
                ).wait_send()
        for level in range(ZROUNDS + 1):
            d = 1 << level
            sent = (z + wide < nz) if level == ZROUNDS else (z < d)

            @pl.when(sent)
            def _():
                push(
                    hvec.at[it, 1 + level], hgot.at[it],
                    h_send.at[it, level], h_recv.at[it],
                    tm=me,
                ).wait_send()

    out_ref[...] = current
    stepped = cell(prev)[5]
    sums.append(jnp.sum(weight * (current - stepped) ** 2, axis=0, keepdims=True))
    total = jnp.concatenate(sums + [jnp.zeros((8 - ITERS, H), F32)], axis=0)

    def exchange(total, part, send, recv, mine, peers, place):
        part[mine] = total
        sent = []
        for j in range(1, peers):
            copy = push(
                part.at[mine], part.at[mine], send.at[j], recv.at[mine],
                **place((mine + j) % peers),
            )
            copy.start()
            sent.append(copy)
        for j in range(1, peers):
            other = (mine + j) % peers
            push(
                part.at[other], part.at[other], send.at[j], recv.at[other],
                **place(other),
            ).wait_recv()
        for copy in sent:
            copy.wait_send()
        total = part[0]
        for j in range(1, peers):
            total = total + part[j]
        return total

    total = exchange(
        total, part_a, a_send, a_recv, inner, PLANE,
        lambda other: {"tm": z * PLANE + other},
    )
    total = exchange(
        total, part_b, b_send, b_recv, col, nx, lambda other: {"batch": other}
    )
    total = exchange(
        total, part_c, c_send, c_recv, z, nz,
        lambda other: {"tm": other * PLANE + inner},
    )
    denom = nx * H * (steps * nz * PLANE + 1) / 2.0
    norms = jnp.sqrt(jnp.sum(total, axis=1, keepdims=True) / denom + 1e-06)
    for k in range(ITERS):
        norm_ref[k] = norms[k, 0]


def per_device(
    nz, nx, inputs, h_start, in_weight, rec_weight, update_bias, reset_bias,
    cand_bias, rec_bias,
):
    steps = inputs.shape[0]
    length = steps // BLOCKS
    vmem = pl.BlockSpec(memory_space=pltpu.VMEM)
    dma = pltpu.SemaphoreType.DMA
    states, norms = pl.pallas_call(
        functools.partial(kernel, nz, nx),
        out_shape=(
            jax.ShapeDtypeStruct((steps, H), F32),
            jax.ShapeDtypeStruct((ITERS,), F32),
        ),
        in_specs=[vmem] * 8,
        out_specs=(vmem, pl.BlockSpec(memory_space=pltpu.SMEM)),
        scratch_shapes=[
            pltpu.VMEM((steps, 3 * H), F32),
            pltpu.VMEM((4, steps, H), F32),
            pltpu.VMEM((steps, H), F32),
            pltpu.VMEM((BLOCKS, length, ROWS, H), F32),
            pltpu.VMEM((ITERS, 3, ROWS, H), F32),
            pltpu.VMEM((ITERS, 3, ROWS, H), F32),
            pltpu.VMEM((1 + BLOCKS, ROWS, H), F32),
            pltpu.VMEM((ITERS, ZROUNDS + 1, ROWS, H), F32),
            pltpu.VMEM((ITERS, max(ZROUNDS, 1), ROWS, H), F32),
            pltpu.VMEM((ITERS, ZROUNDS + 2, 8, H), F32),
            pltpu.VMEM((ITERS, 8, H), F32),
            pltpu.VMEM((8 + steps, H), F32),
            pltpu.VMEM((BLOCKS, ROWS, H), F32),
            pltpu.VMEM((PLANE, 8, H), F32),
            pltpu.VMEM((nx, 8, H), F32),
            pltpu.VMEM((nz, 8, H), F32),
            dma((ITERS, 3)), dma((ITERS, 3)),
            dma((ITERS, max(ZROUNDS, 1))), dma((ITERS, max(ZROUNDS, 1))),
            dma((ITERS, ZROUNDS + 1)), dma((ITERS,)),
            dma((PLANE,)), dma((PLANE,)),
            dma((nx,)), dma((nx,)),
            dma((nz,)), dma((nz,)),
        ],
        compiler_params=pltpu.CompilerParams(collective_id=0, has_side_effects=True),
        name="deer",
    )(
        inputs.reshape(steps, -1), h_start, in_weight, rec_weight,
        update_bias.reshape(1, H), reset_bias.reshape(1, H),
        cand_bias.reshape(1, H), rec_bias.reshape(1, H),
    )
    return states.reshape(steps, 1, H), norms


def solution(mesh):
    nz = mesh.shape["tm"] // PLANE
    nx = mesh.shape["batch"]
    in_specs = (P("tm", "batch", None), P("batch", None), P(), P(), P(), P(), P(), P())
    out_specs = (P("tm", "batch", None), P())
    return jax.shard_map(
        functools.partial(per_device, nz, nx), mesh=mesh, in_specs=in_specs,
        out_specs=out_specs, check_vma=False,
    )
```

time: 2300 us -> 92 us (0.04)
  starting transfers between devices: 1780 us -> 0 us
  blocking collectives: 250 us -> 0 us
  waiting for transfers between devices: 185 us -> 0 us
  Pallas kernels: 0 us -> 89.3 us
  matrix products: 63.5 us -> 0 us
    ppermute x258 -> x0, starting transfers between devices: 1780 us -> none  [passed_along(): return lax.ppermute(shard, axis, pairs)]
    psum x1 -> x0, blocking collectives: 250 us -> none  [record(): return lax.psum(local_sum, ('tm', 'batch'))]
    ppermute x258 -> x0, waiting for transfers between devices: 185 us -> none  [passed_along(): return lax.ppermute(shard, axis, pairs)]
    pallas_call x0 -> x1, Pallas kernels: none -> 89.3 us  [per_device(): pl.pallas_call(functools.partial(kernel, nz, nx), out_shape=(jax.ShapeDty...]
    dot_general x316 -> x0, matrix products: 63.5 us -> none  [the longest x256 39.3 us: relay(): leaving = jnp.dot(carried, whole_mat, precision=HIGH) + whole_vec]
  transfers between devices with their start and end apart: 258 -> 0, of which waited for: 258 -> 0; matrix products, arithmetic and copies ran while one was open for 0% -> 0% of each run, Pallas kernels for 0% -> 0%
where the time goes in v1:
time: 92 us; the launch traced here: 91.8 us
  Pallas kernels  89.3 us (97%)
  local copies, waits for them, and re-layouts  1.84 us (2%)
    pallas_call x1, Pallas kernels, per_device(): pl.pallas_call(functools.partial(kernel, nz, nx), out_shape=(jax.ShapeDty...  89.3 us
    unnamed x4, local copies, waits for them, and re-layouts  1.84 us

profile of v1, /device:TPU:1, one launch (start us, length us, event | category | flops | bytes accessed | tf_op | source)
XLA Modules:
  0.0 91.8 jit_solution(16723526547694907738)
XLA Ops:
  0.6 89.3 %deer.1 = (f32[32,128]{1,0:T(8,128)}, f32[2]{0:T(128)}) custom-call(bf16[32,128]{1,0:T(8,128)(2,1)} %bitcast.9, f32[1,128]{1,0:T(1,128)} %start_ref.1, bf16[128,384]{1,0:T(8,128)(2,1)} %in_w_ref.1, f32[128,384]{1,0:T(8,128)} %rec_w_ref.1, f32[1,128]{1,0:T(1,128)} %bitcast.10, f32[1,128]{1,0:T(1,128)} %bitcast.11, f32[1,128]{1,0:T(1,128)} %bitcast.12, ...), custom_call_target="tpu_custom_call" | custom-call | tf_op jit(solution)/shard_map/deer/pallas_call | solution.py:368
  89.9 0.0 copy-start
  89.9 1.3 %copy.13 = f32[32,1,128]{2,1,0:T(1,128)} copy(f32[32,1,128]{2,1,0:T(1,128)} %bitcast.8) | data formatting | bytes 32768
  91.3 0.0 copy-done
  91.3 0.5 copy.14
Async XLA Ops:
  89.9 1.3 %copy-start = (f32[2]{0:T(128)S(1)}, f32[2]{0:T(128)}, u32[]{:S(2)}) copy-start(f32[2]{0:T(128)} %get-tuple-element.11) | copy-start | bytes 28

commit v2 on v1

--- a/solution.py
+++ b/solution.py
@@ -8,7 +8,8 @@
 
 ITERS = 2
 BLOCKS = 4
-PLANE = 8
+YS = 4
+PLANE = 2 * YS
 ZROUNDS = 1
 H = 128
 ROWS = H + 8
@@ -43,9 +44,9 @@
     nz, nx,
     x_ref, start_ref, in_w_ref, rec_w_ref, ub_ref, rb_ref, cb_ref, nb_ref,
     out_ref, norm_ref,
-    gx, coef, offs, prefix, own, got, acc, zown, zgot, hvec, hgot, hbuf, heads,
-    part_a, part_b, part_c,
-    m_send, m_recv, z_send, z_recv, h_send, h_recv,
+    gx, coef, offs, prefix, own, got, chips, lead, acc, zown, zgot, hvec, hgot, hbuf,
+    heads, part_a, part_b, part_c, reach,
+    m_send, m_recv, y_send, y_recv, z_send, z_recv, h_send, h_recv,
     a_send, a_recv, b_send, b_recv, c_send, c_recv,
 ):
     steps = x_ref.shape[0]
@@ -57,26 +58,33 @@
     y = inner // 2
     core = inner % 2
 
-    mates = (
-        z * PLANE + y * 2 + (1 - core),
-        z * PLANE + (y + 1 - 2 * (y % 2)) * 2 + core,
-        z * PLANE + (3 - y) * 2 + core,
-    )
-    uppers = (core == 1, y % 2 == 1, y >= 2)
+    twin = z * PLANE + y * 2 + (1 - core)
+
+    def along_y(j):
+        return z * PLANE + ((y + j) % YS) * 2 + core
+
+    def along_z(j):
+        return ((z + j) % nz) * PLANE + inner
+
+    others = sorted(
+        ((j, i) for j in range(YS) for i in range(nx) if i or j),
+        key=lambda ji: -min(ji[0], YS - ji[0]) - min(ji[1], nx - ji[1]),
+    )
+    far_z = sorted(range(1, nz), key=lambda j: -min(j, nz - j))
 
     barrier = pltpu.get_barrier_semaphore()
 
-    def hello(**where):
+    def hello(sem, **where):
         pl.semaphore_signal(
-            barrier, inc=1, device_id=where, device_id_type=pl.DeviceIdType.MESH
+            sem, inc=1, device_id=where, device_id_type=pl.DeviceIdType.MESH
         )
 
-    for j in range(1, PLANE):
-        hello(tm=z * PLANE + (inner + j) % PLANE)
-    for j in range(1, nz):
-        hello(tm=((z + j) % nz) * PLANE + inner)
-    for j in range(1, nx):
-        hello(batch=(col + j) % nx)
+    near = [-2, -1, 1, 2]
+    hello(barrier, tm=twin)
+    for j in near:
+        hello(barrier, tm=along_z(j))
+    for j, i in others:
+        hello(barrier, tm=along_y(j), batch=(col + i) % nx)
 
     eye = (
         lax.broadcasted_iota(jnp.int32, (H, H), 0)
@@ -160,45 +168,57 @@
             prefix[b, 0, H:] = step_tail(b * length)
 
         def extend(t, carry):
+            before = [prefix[b, t - 1] for b in range(BLOCKS)]
+            late = [step_matrix(b * length + t) for b in range(BLOCKS)]
+            tail = [step_tail(b * length + t) for b in range(BLOCKS)]
+            more = [split_dot(before[b], late[b]) for b in range(BLOCKS)]
             for b in range(BLOCKS):
-                before = prefix[b, t - 1]
-                late = step_matrix(b * length + t)
-                more = split_dot(before, late)
-                prefix[b, t, :H] = before[:H] + late + more[:H]
-                prefix[b, t, H:] = before[H:] + step_tail(b * length + t) + more[H:]
+                prefix[b, t, :H] = before[b][:H] + late[b] + more[b][:H]
+                prefix[b, t, H:] = before[b][H:] + tail[b] + more[b][H:]
             return carry
 
-        lax.fori_loop(1, length, extend, 0)
+        lax.fori_loop(1, length, extend, 0, unroll=True)
 
         last = length - 1
-        heads[1] = prefix[0, last]
-        heads[2] = compose(prefix[0, last], prefix[1, last])
-        tail_pair = compose(prefix[2, last], prefix[3, last])
-        own[it, 0] = compose(heads[2], tail_pair)
-
+        ends = [prefix[b, last] for b in range(BLOCKS)]
+        head_pair = compose(ends[0], ends[1])
+        whole = compose(head_pair, compose(ends[2], ends[3]))
+        own[it] = whole
         if it == 0:
-            pl.semaphore_wait(barrier, (PLANE - 1) + (nz - 1) + (nx - 1))
-
-        copies = []
-        for k in range(3):
+            pl.semaphore_wait(barrier, 1 + len(near) + len(others))
+            for j in (-2, 2):
+                hello(reach.at[0], tm=along_z(j))
+        pair_copy = push(own.at[it], got.at[it], m_send.at[it], m_recv.at[it], tm=twin)
+        pair_copy.start()
+        heads[0] = ends[0]
+        heads[1] = head_pair
+        heads[2] = compose(head_pair, ends[2])
+        pair_copy.wait_recv()
+        theirs = got[it]
+        early = jnp.where(core == 1, theirs, whole)
+        late = jnp.where(core == 1, whole, theirs)
+        chips[it, y] = compose(early, late)
+        chip_copies = []
+        for j in (2, 1, 3):
             copy = push(
-                own.at[it, k], got.at[it, k], m_send.at[it, k], m_recv.at[it, k],
-                tm=mates[k],
+                chips.at[it, y], chips.at[it, y], y_send.at[it, j], y_recv.at[it, y],
+                tm=along_y(j),
             )
             copy.start()
-            copies.append(copy)
-            if k == 0:
-                heads[3] = compose(heads[2], prefix[2, last])
-            copy.wait_recv()
-            mine = own[it, k]
-            theirs = got[it, k]
-            early = jnp.where(uppers[k], theirs, mine)
-            late = jnp.where(uppers[k], mine, theirs)
-            merged = compose(early, late)
-            if k < 2:
-                own[it, k + 1] = merged
-            else:
-                zown[it, 0] = merged
+            chip_copies.append(copy)
+        if it == 0:
+            pl.semaphore_wait(reach.at[0], 2)
+            for j in (-4, 4):
+                hello(reach.at[1], tm=along_z(j))
+        for j in (1, 3, 2):
+            source = (y + j) % YS
+            push(
+                chips.at[it, source], chips.at[it, source],
+                y_send.at[it, j], y_recv.at[it, source], tm=along_y(j),
+            ).wait_recv()
+        parts = [chips[it, j] for j in range(YS)]
+        low_pair = compose(parts[0], parts[1])
+        zown[it, 0] = compose(low_pair, compose(parts[2], parts[3]))
 
         h_copy_out = []
 
@@ -253,14 +273,18 @@
         wide = 1 << ZROUNDS
         known = 1 if ZROUNDS == 0 else wide // 2
 
-        zero = jnp.zeros((ROWS, H), F32)
-
         def inner_map():
-            lead = jnp.where(uppers[2], got[it, 2], zero)
-            acc[0] = compose(lead, jnp.where(uppers[1], got[it, 1], zero))
-            acc[1] = compose(acc[0], jnp.where(uppers[0], got[it, 0], zero))
-            for b in range(1, BLOCKS):
-                acc[1 + b] = compose(acc[1], heads[b])
+            lead[0] = jnp.zeros((ROWS, H), F32)
+            lead[1] = parts[0]
+            lead[2] = low_pair
+            lead[3] = compose(low_pair, parts[2])
+            first_map = compose(
+                lead[y], jnp.where(core == 1, theirs, jnp.zeros((ROWS, H), F32))
+            )
+            rest = [compose(first_map, heads[b]) for b in range(BLOCKS - 1)]
+            acc[0] = first_map
+            for b in range(BLOCKS - 1):
+                acc[1 + b] = rest[b]
 
         @pl.when(z < known)
         def _():
@@ -278,10 +302,10 @@
         relay(wide, ZROUNDS, (z >= known) & (z + wide < nz))
 
         entering = hvec[it, 0]
-        at_device = apply(entering, acc[1])
+        at_device = apply(entering, acc[0])
         hbuf[0:8] = at_device
         for b in range(BLOCKS):
-            head = at_device if b == 0 else apply(entering, acc[1 + b])
+            head = at_device if b == 0 else apply(entering, acc[b])
             column = jnp.sum(eye * head[:1], axis=1, keepdims=True)
             rows = []
             for t in range(length):
@@ -291,8 +315,10 @@
         current = hbuf[8 : 8 + steps]
         prev = hbuf[7 : 7 + steps]
 
-        for k in range(3):
-            copies[k].wait_send()
+        if it == 0:
+            pl.semaphore_wait(reach.at[1], 2)
+        for copy in [pair_copy] + chip_copies:
+            copy.wait_send()
         for k, d in enumerate(z_out):
             @pl.when(z >= d)
             def _():
@@ -317,39 +343,40 @@
     sums.append(jnp.sum(weight * (current - stepped) ** 2, axis=0, keepdims=True))
     total = jnp.concatenate(sums + [jnp.zeros((8 - ITERS, H), F32)], axis=0)
 
-    def exchange(total, part, send, recv, mine, peers, place):
+    def exchange(total, part, send, recv, mine, peers):
         part[mine] = total
         sent = []
-        for j in range(1, peers):
-            copy = push(
-                part.at[mine], part.at[mine], send.at[j], recv.at[mine],
-                **place((mine + j) % peers),
-            )
+        for j, (_, where) in enumerate(peers):
+            copy = push(part.at[mine], part.at[mine], send.at[j], recv.at[mine], **where)
             copy.start()
             sent.append(copy)
-        for j in range(1, peers):
-            other = (mine + j) % peers
+        for j, (other, where) in enumerate(peers):
             push(
-                part.at[other], part.at[other], send.at[j], recv.at[other],
-                **place(other),
+                part.at[other], part.at[other], send.at[j], recv.at[other], **where
             ).wait_recv()
         for copy in sent:
             copy.wait_send()
         total = part[0]
-        for j in range(1, peers):
+        for j in range(1, len(peers) + 1):
             total = total + part[j]
         return total
 
     total = exchange(
-        total, part_a, a_send, a_recv, inner, PLANE,
-        lambda other: {"tm": z * PLANE + other},
+        total, part_a, a_send, a_recv, core, [(1 - core, {"tm": twin})]
     )
     total = exchange(
-        total, part_b, b_send, b_recv, col, nx, lambda other: {"batch": other}
+        total, part_b, b_send, b_recv, y * nx + col,
+        [
+            (
+                (y + j) % YS * nx + (col + i) % nx,
+                {"tm": along_y(j), "batch": (col + i) % nx},
+            )
+            for j, i in others
+        ],
     )
     total = exchange(
-        total, part_c, c_send, c_recv, z, nz,
-        lambda other: {"tm": other * PLANE + inner},
+        total, part_c, c_send, c_recv, z,
+        [((z + j) % nz, {"tm": along_z(j)}) for j in far_z],
     )
     denom = nx * H * (steps * nz * PLANE + 1) / 2.0
     norms = jnp.sqrt(jnp.sum(total, axis=1, keepdims=True) / denom + 1e-06)
@@ -378,23 +405,27 @@
             pltpu.VMEM((4, steps, H), F32),
             pltpu.VMEM((steps, H), F32),
             pltpu.VMEM((BLOCKS, length, ROWS, H), F32),
-            pltpu.VMEM((ITERS, 3, ROWS, H), F32),
-            pltpu.VMEM((ITERS, 3, ROWS, H), F32),
-            pltpu.VMEM((1 + BLOCKS, ROWS, H), F32),
+            pltpu.VMEM((ITERS, ROWS, H), F32),
+            pltpu.VMEM((ITERS, ROWS, H), F32),
+            pltpu.VMEM((ITERS, YS, ROWS, H), F32),
+            pltpu.VMEM((YS, ROWS, H), F32),
+            pltpu.VMEM((BLOCKS, ROWS, H), F32),
             pltpu.VMEM((ITERS, ZROUNDS + 1, ROWS, H), F32),
             pltpu.VMEM((ITERS, max(ZROUNDS, 1), ROWS, H), F32),
             pltpu.VMEM((ITERS, ZROUNDS + 2, 8, H), F32),
             pltpu.VMEM((ITERS, 8, H), F32),
             pltpu.VMEM((8 + steps, H), F32),
-            pltpu.VMEM((BLOCKS, ROWS, H), F32),
-            pltpu.VMEM((PLANE, 8, H), F32),
-            pltpu.VMEM((nx, 8, H), F32),
+            pltpu.VMEM((BLOCKS - 1, ROWS, H), F32),
+            pltpu.VMEM((2, 8, H), F32),
+            pltpu.VMEM((YS * nx, 8, H), F32),
             pltpu.VMEM((nz, 8, H), F32),
-            dma((ITERS, 3)), dma((ITERS, 3)),
+            pltpu.SemaphoreType.REGULAR((2,)),
+            dma((ITERS,)), dma((ITERS,)),
+            dma((ITERS, YS)), dma((ITERS, YS)),
             dma((ITERS, max(ZROUNDS, 1))), dma((ITERS, max(ZROUNDS, 1))),
             dma((ITERS, ZROUNDS + 1)), dma((ITERS,)),
-            dma((PLANE,)), dma((PLANE,)),
-            dma((nx,)), dma((nx,)),
+            dma((1,)), dma((2,)),
+            dma((YS * nx,)), dma((YS * nx,)),
             dma((nz,)), dma((nz,)),
         ],
         compiler_params=pltpu.CompilerParams(collective_id=0, has_side_effects=True),

time: 92 us -> 80.6 us (0.88)
  Pallas kernels: 89.3 us -> 77.9 us
    pallas_call x1, Pallas kernels: 89.3 us -> 77.9 us  [per_device(): pl.pallas_call(functools.partial(kernel, nz, nx), out_shape=(jax.ShapeDty...]
where the time goes in v2:
time: 80.6 us; the launch traced here: 80.4 us
  Pallas kernels  77.9 us (97%)
  local copies, waits for them, and re-layouts  1.84 us (2%)
    pallas_call x1, Pallas kernels, per_device(): pl.pallas_call(functools.partial(kernel, nz, nx), out_shape=(jax.ShapeDty...  77.9 us
    unnamed x4, local copies, waits for them, and re-layouts  1.84 us

profile of v2, /device:TPU:1, one launch (start us, length us, event | category | flops | bytes accessed | tf_op | source)
XLA Modules:
  0.0 80.4 jit_solution(4620954197470749126)
XLA Ops:
  0.6 77.9 %deer.1 = (f32[32,128]{1,0:T(8,128)}, f32[2]{0:T(128)}) custom-call(bf16[32,128]{1,0:T(8,128)(2,1)} %bitcast.9, f32[1,128]{1,0:T(1,128)} %start_ref.1, bf16[128,384]{1,0:T(8,128)(2,1)} %in_w_ref.1, f32[128,384]{1,0:T(8,128)} %rec_w_ref.1, f32[1,128]{1,0:T(1,128)} %bitcast.10, f32[1,128]{1,0:T(1,128)} %bitcast.11, f32[1,128]{1,0:T(1,128)} %bitcast.12, ...), custom_call_target="tpu_custom_call" | custom-call | tf_op jit(solution)/shard_map/deer/pallas_call | solution.py:395
  78.6 0.0 copy-start
  78.6 1.3 %copy.13 = f32[32,1,128]{2,1,0:T(1,128)} copy(f32[32,1,128]{2,1,0:T(1,128)} %bitcast.8) | data formatting | bytes 32768
  79.9 0.0 copy-done
  79.9 0.5 copy.14
Async XLA Ops:
  78.6 1.3 %copy-start = (f32[2]{0:T(128)S(1)}, f32[2]{0:T(128)}, u32[]{:S(2)}) copy-start(f32[2]{0:T(128)} %get-tuple-element.11) | copy-start | bytes 28
